TPU v7x, 32 devices: a whole 2x2x4 slice. The times are simulated.
32 devices in a mesh: vocab: 4 (over x, core), fsdp: 8 (over z, y).
Axes of the slice: x: 2, y: 2, z: 4, core: 2. Of those that a mesh axis runs over, the one named last changes fastest.
Arguments:
- hidden: bfloat16 [2, 384, 4096], P(None, 'fsdp'), may hold values from -1000 to 1000
- norm_gain: bfloat16 [4096], replicated, may hold values from 0.5 to 1.5
- labels: int32 [2, 384], P(None, 'fsdp'), may hold values from 0 to 65535
- head_weight: bfloat16 [4096, 65536], P(None, ('vocab', 'fsdp')), may hold values from -1 to 1
- head_ema: float32 [4096, 65536], P(None, ('vocab', 'fsdp')), may hold values from 1e-09 to 0.001
- gain_ema: float32 [4096], replicated, may hold values from 0.0001 to 0.03
Outputs:
- head_ema_new: float32 [4096, 65536], P(None, ('vocab', 'fsdp'))
- gain_ema_new: float32 [4096], replicated
All inputs are finite; a program needn't handle non-finite values.
Results may differ from a plain program's by a relative error of at most 0.00049.
Values may be sent and summed in bfloat16 or wider, within the bound.
A program may use at most 192 MiB of HBM per device.

v0:
```python
import functools

import jax
import jax.numpy as jnp
from jax import lax
from jax.experimental import pallas as pl
from jax.experimental.pallas import tpu as pltpu
from jax.sharding import PartitionSpec as P

BETA = 0.99
EPS = 1e-05
LANES = 128
MESH = pl.DeviceIdType.MESH
VMEM_LIMIT = 60 * 1024 * 1024


def normalize_kernel(hidden_ref, gain_ref, scaled_ref):
    wide = hidden_ref[...].astype(jnp.float32)
    factor = lax.rsqrt(jnp.mean(wide * wide, axis=-1, keepdims=True) + EPS)
    scaled_ref[...] = (wide * factor * gain_ref[...].astype(jnp.float32)).astype(jnp.bfloat16)


def bits_of(size):
    return [1 << place for place in reversed(range(size.bit_length() - 1))]


def flip(index, mask):
    for place in range(mask.bit_length()):
        bit = 1 << place
        if mask & bit:
            index = index + bit - 2 * bit * lax.rem(lax.div(index, bit), 2)
    return index


def shared_width(features, ways):
    return features // 8 // LANES * LANES if ways == 4 else 0


def gather_sends(parts, ways, features):
    return (parts - 1) * (ways + (2 if shared_width(features, ways) else 0))


def gather_kernel(parts, ways, own_ref, all_ref, send_sem, recv_sem, local_sem):
    part, way = lax.axis_index("fsdp"), lax.axis_index("vocab")
    features = own_ref.shape[1]
    both = shared_width(features, ways)
    single = (features - 2 * both) // ways
    part_bits, way_bits = bits_of(parts), bits_of(ways)

    barrier = pltpu.get_barrier_semaphore()
    for bit in part_bits:
        pl.semaphore_signal(barrier, inc=1, device_id=(way, flip(part, bit)), device_id_type=MESH)
    for bit in way_bits:
        pl.semaphore_signal(barrier, inc=1, device_id=(flip(way, bit), part), device_id_type=MESH)
    pl.semaphore_wait(barrier, len(part_bits) + len(way_bits))

    kinds = ([("both", [1])] if both else []) + [("single", way_bits)]

    def columns(kind, piece_mask):
        piece = flip(way, piece_mask)
        if kind == "both":
            return pl.ds(pl.multiple_of(single * ways + lax.rem(piece, 2) * both, LANES), both)
        return pl.ds(pl.multiple_of(piece * single, LANES), single)

    def slot(kind, part_mask, piece_mask):
        return (part_mask - 1) * (ways + 2) + (ways if kind == "both" else 0) + piece_mask

    sends = []

    def send(kind, part_mask, piece_mask, part_bit, way_bit):
        where = columns(kind, piece_mask)
        shard = flip(part, part_mask)
        target = all_ref.at[shard, :, where]
        copy = pltpu.make_async_remote_copy(
            src_ref=target if part_mask else own_ref.at[:, where],
            dst_ref=target,
            send_sem=send_sem.at[len(sends)],
            recv_sem=recv_sem.at[slot(kind, part_mask ^ part_bit, piece_mask ^ way_bit)],
            device_id=(flip(way, way_bit), flip(part, part_bit)),
            device_id_type=MESH,
        )
        copy.start()
        sends.append(copy)

    def forward(kind, kind_bits, part_mask, piece_mask):
        if not piece_mask:
            for bit in part_bits:
                if not part_mask or bit < part_mask & -part_mask:
                    send(kind, part_mask, 0, bit, 0)
        if part_mask:
            for bit in kind_bits:
                if not piece_mask or bit < piece_mask & -piece_mask:
                    send(kind, part_mask, piece_mask, 0, bit)

    def arrive(kind, part_mask, piece_mask):
        target = all_ref.at[flip(part, part_mask), :, columns(kind, piece_mask)]
        pltpu.make_async_remote_copy(
            src_ref=target,
            dst_ref=target,
            send_sem=send_sem.at[0],
            recv_sem=recv_sem.at[slot(kind, part_mask, piece_mask)],
            device_id=(flip(way, way_bits[-1]), part),
            device_id_type=MESH,
        ).wait_recv()

    keep = pltpu.make_async_copy(own_ref, all_ref.at[part], local_sem)
    for kind, kind_bits in reversed(kinds):
        forward(kind, kind_bits, 0, 0)
    keep.start()
    order = sorted(range(1, parts), key=lambda mask: (mask.bit_count(), -mask))
    for part_mask in order:
        for kind, kind_bits in reversed(kinds):
            arrive(kind, part_mask, 0)
            forward(kind, kind_bits, part_mask, 0)
    for last in (False, True):
        for part_mask in order:
            for kind, kind_bits in reversed(kinds):
                for piece_mask in range(1, 2 * kind_bits[0]):
                    if (piece_mask % 2 == 1) == last:
                        arrive(kind, part_mask, piece_mask)
                        forward(kind, kind_bits, part_mask, piece_mask)
    for copy in sends:
        copy.wait_send()
    keep.wait()


def gather_rows(own, parts, ways):
    rows, features = own.shape
    sends = gather_sends(parts, ways, features)
    return pl.pallas_call(
        functools.partial(gather_kernel, parts, ways),
        out_shape=jax.ShapeDtypeStruct((parts, rows, features), own.dtype),
        in_specs=[pl.BlockSpec(memory_space=pltpu.VMEM)],
        out_specs=pl.BlockSpec(memory_space=pl.ANY),
        scratch_shapes=[
            pltpu.SemaphoreType.DMA((sends,)),
            pltpu.SemaphoreType.DMA(((parts - 1) * (ways + 2),)),
            pltpu.SemaphoreType.DMA,
        ],
        compiler_params=pltpu.CompilerParams(collective_id=0, has_side_effects=True),
        name="gather_rows",
    )(own)


def exchange_kernel(parts, ways, combine, x_ref, y_ref, part_slots, way_slots, half, send_sem, part_sem, way_sem):
    part, way = lax.axis_index("fsdp"), lax.axis_index("vocab")
    barrier = pltpu.get_barrier_semaphore()
    for step in range(1, parts):
        pl.semaphore_signal(barrier, inc=1, device_id=(way, lax.rem(part + step, parts)), device_id_type=MESH)
    for step in range(1, ways):
        pl.semaphore_signal(barrier, inc=1, device_id=(lax.rem(way + step, ways), part), device_id_type=MESH)
    pl.semaphore_wait(barrier, parts + ways - 2)

    copies = []
    for step in range(1, parts):
        copies.append(
            pltpu.make_async_remote_copy(
                src_ref=x_ref,
                dst_ref=part_slots.at[part],
                send_sem=send_sem.at[step - 1],
                recv_sem=part_sem.at[step - 1],
                device_id=(way, lax.rem(part + step, parts)),
                device_id_type=MESH,
            )
        )
        copies[-1].start()
    part_slots[part] = x_ref[...]
    for step in range(1, parts):
        pltpu.make_async_remote_copy(
            src_ref=x_ref,
            dst_ref=part_slots.at[lax.rem(part + parts - step, parts)],
            send_sem=send_sem.at[step - 1],
            recv_sem=part_sem.at[step - 1],
            device_id=(way, lax.rem(part + step, parts)),
            device_id_type=MESH,
        ).wait_recv()
    half[...] = combine([part_slots[index] for index in range(parts)], False)
    for step in range(1, ways):
        copies.append(
            pltpu.make_async_remote_copy(
                src_ref=half,
                dst_ref=way_slots.at[way],
                send_sem=send_sem.at[parts - 2 + step],
                recv_sem=way_sem.at[step - 1],
                device_id=(lax.rem(way + step, ways), part),
                device_id_type=MESH,
            )
        )
        copies[-1].start()
    way_slots[way] = half[...]
    for step in range(1, ways):
        pltpu.make_async_remote_copy(
            src_ref=half,
            dst_ref=way_slots.at[lax.rem(way + ways - step, ways)],
            send_sem=send_sem.at[parts - 2 + step],
            recv_sem=way_sem.at[step - 1],
            device_id=(lax.rem(way + step, ways), part),
            device_id_type=MESH,
        ).wait_recv()
    y_ref[...] = combine([way_slots[index] for index in range(ways)], True)
    for copy in copies:
        copy.wait_send()


def exchange(x, parts, ways, combine, number, name):
    return pl.pallas_call(
        functools.partial(exchange_kernel, parts, ways, combine),
        out_shape=jax.ShapeDtypeStruct(x.shape, x.dtype),
        in_specs=[pl.BlockSpec(memory_space=pltpu.VMEM)],
        out_specs=pl.BlockSpec(memory_space=pltpu.VMEM),
        scratch_shapes=[
            pltpu.VMEM((parts,) + x.shape, x.dtype),
            pltpu.VMEM((ways,) + x.shape, x.dtype),
            pltpu.VMEM(x.shape, x.dtype),
            pltpu.SemaphoreType.DMA((parts + ways - 2,)),
            pltpu.SemaphoreType.DMA((parts - 1,)),
            pltpu.SemaphoreType.DMA((ways - 1,)),
        ],
        compiler_params=pltpu.CompilerParams(collective_id=number, has_side_effects=True),
        name=name,
    )(x)


def combine_stats(terms, labels_done):
    top = functools.reduce(jnp.maximum, [term[0:1] for term in terms])
    total = sum(term[1:2] * jnp.exp(term[0:1] - top) for term in terms)
    label = terms[0][2:3] if labels_done else sum(term[2:3] for term in terms)
    return jnp.concatenate([top, total, label, jnp.zeros((1, top.shape[1]), jnp.float32)], axis=0)


def combine_sum(terms, labels_done):
    return sum(terms)


def logits_kernel(rows_ref, weight_ref, label_ref, logits_ref, stats_ref, top_ref, total_ref):
    step = pl.program_id(0)

    @pl.when(step == 0)
    def _():
        top_ref[...] = jnp.full_like(top_ref, -jnp.inf)
        total_ref[...] = jnp.zeros_like(total_ref)

    logits_ref[...] = jnp.dot(rows_ref[...], weight_ref[...], preferred_element_type=jnp.float32)
    groups = [logits_ref[:, start : start + LANES] for start in range(0, logits_ref.shape[1], LANES)]
    old = top_ref[...]
    top = functools.reduce(jnp.maximum, groups, old)
    total_ref[...] = total_ref[...] * jnp.exp(old - top) + sum(jnp.exp(group - top) for group in groups)
    top_ref[...] = top

    @pl.when(step == pl.num_programs(0) - 1)
    def _():
        wide_top = top_ref[...].T
        row_top = jnp.max(wide_top, axis=0, keepdims=True)
        row_total = jnp.sum(total_ref[...].T * jnp.exp(wide_top - row_top), axis=0, keepdims=True)
        stats_ref[...] = jnp.concatenate(
            [row_top, row_total, label_ref[...], jnp.zeros((1, row_top.shape[1]), jnp.float32)], axis=0
        )


def local_logits(rows_all, head_weight, label_row):
    rows, features = rows_all.shape
    columns = head_weight.shape[1]
    tile = min(256, columns)
    return pl.pallas_call(
        logits_kernel,
        grid=(columns // tile,),
        out_shape=(
            jax.ShapeDtypeStruct((rows, columns), jnp.float32),
            jax.ShapeDtypeStruct((4, rows), jnp.float32),
        ),
        in_specs=[
            pl.BlockSpec((rows, features), lambda i: (0, 0), pipeline_mode=pl.Buffered(1)),
            pl.BlockSpec((features, tile), lambda i: (0, i)),
            pl.BlockSpec((1, rows), lambda i: (0, 0)),
        ],
        out_specs=(pl.BlockSpec((rows, tile), lambda i: (0, i)), pl.BlockSpec((4, rows), lambda i: (0, 0))),
        scratch_shapes=[pltpu.VMEM((rows, LANES), jnp.float32)] * 2,
        compiler_params=pltpu.CompilerParams(vmem_limit_bytes=VMEM_LIMIT),
        name="local_logits",
    )(rows_all, head_weight, label_row)


def update_kernel(
    chunk, rows_ref, stats_ref, logits_ref, weight_ref, ema_ref, new_ref, gain_ref, slope_ref, top_ref, scale_ref, label_ref
):
    count, columns = logits_ref.shape

    @pl.when(pl.program_id(0) == 0)
    def _():
        stats = stats_ref[...]
        top_ref[...] = jnp.broadcast_to(stats[0:1], (LANES, count)).T
        scale_ref[...] = jnp.broadcast_to(1.0 / stats[1:2], (LANES, count)).T
        label_ref[...] = jnp.broadcast_to(stats[2:3], (LANES, count)).T
        first = (lax.axis_index("vocab") * lax.axis_size("fsdp") + lax.axis_index("fsdp")) * columns

        @pl.loop(0, count // chunk)
        def _(index):
            some = pl.ds(pl.multiple_of(index * chunk, chunk), chunk)
            top, scale, label = top_ref[some, :], scale_ref[some, :], label_ref[some, :].astype(jnp.int32)
            label = label - first
            lane = lax.broadcasted_iota(jnp.int32, (chunk, LANES), 1)
            for start in range(0, columns, LANES):
                chances = jnp.exp(logits_ref[some, start : start + LANES] - top) * scale
                hits = (label == lane + start).astype(jnp.float32)
                slope_ref[some, start : start + LANES] = (chances - hits).astype(slope_ref.dtype)

    mix = (1.0 - BETA) / count
    tall = rows_ref[...].T
    total = jnp.zeros((tall.shape[0], LANES), jnp.float32)
    width = min(512, columns)
    for start in range(0, columns, width):
        gradient = jnp.dot(tall, slope_ref[:, start : start + width], preferred_element_type=jnp.float32)
        new_ref[:, start : start + width] = BETA * ema_ref[:, start : start + width] + mix * gradient * gradient
        product = weight_ref[:, start : start + width].astype(jnp.float32) * gradient
        for lane in range(0, width, LANES):
            total = total + product[:, lane : lane + LANES]
    gain_ref[...] = jnp.sum(total.T, axis=0, keepdims=True)


def head_update(rows_all, stats, logits, head_weight, head_ema, chunk):
    rows, features = rows_all.shape
    columns = head_weight.shape[1]
    tile = 512 if features % 512 == 0 else 256
    once = dict(pipeline_mode=pl.Buffered(1))
    return pl.pallas_call(
        functools.partial(update_kernel, chunk),
        grid=(features // tile,),
        out_shape=(
            jax.ShapeDtypeStruct((features, columns), jnp.float32),
            jax.ShapeDtypeStruct((1, features), jnp.float32),
        ),
        in_specs=[
            pl.BlockSpec((rows, tile), lambda i: (0, i)),
            pl.BlockSpec((4, rows), lambda i: (0, 0)),
            pl.BlockSpec((rows, columns), lambda i: (0, 0), **once),
            pl.BlockSpec((tile, columns), lambda i: (i, 0)),
            pl.BlockSpec((tile, columns), lambda i: (i, 0)),
        ],
        out_specs=(pl.BlockSpec((tile, columns), lambda i: (i, 0)), pl.BlockSpec((1, tile), lambda i: (0, i))),
        scratch_shapes=[pltpu.VMEM((rows, columns), jnp.bfloat16)] + [pltpu.VMEM((rows, LANES), jnp.float32)] * 3,
        compiler_params=pltpu.CompilerParams(vmem_limit_bytes=VMEM_LIMIT),
        name="head_update",
    )(rows_all, stats, logits, head_weight, head_ema)


def on_device(parts, ways, hidden, norm_gain, labels, head_weight, head_ema, gain_ema):
    batches, own_rows, features = hidden.shape
    own = batches * own_rows
    count = own * parts
    gain_wide = norm_gain.astype(jnp.float32)
    scaled = pl.pallas_call(
        normalize_kernel,
        out_shape=jax.ShapeDtypeStruct((own, features), jnp.bfloat16),
        name="normalize",
    )(hidden.reshape(own, features), norm_gain.reshape(1, features))
    mine = lax.iota(jnp.int32, parts)[:, None] == lax.axis_index("fsdp")
    label_row = jnp.where(mine, labels.reshape(1, own).astype(jnp.float32), 0.0).reshape(1, count)

    rows_all = gather_rows(scaled, parts, ways).reshape(count, features)
    logits, stats = local_logits(rows_all, head_weight, label_row)
    stats = exchange(stats, parts, ways, combine_stats, 1, "exchange_stats")
    head_new, partial_sum = head_update(rows_all, stats, logits, head_weight, head_ema, own)
    gain_grad = exchange(partial_sum, parts, ways, combine_sum, 2, "exchange_gain").reshape(features) / gain_wide
    gain_new = BETA * gain_ema + (1.0 - BETA) * gain_grad * gain_grad / count
    return (head_new, gain_new)


def solution(mesh):
    return jax.shard_map(
        functools.partial(on_device, mesh.shape["fsdp"], mesh.shape["vocab"]),
        mesh=mesh,
        in_specs=(
            P(None, "fsdp", None),
            P(),
            P(None, "fsdp"),
            P(None, ("vocab", "fsdp")),
            P(None, ("vocab", "fsdp")),
            P(),
        ),
        out_specs=(P(None, ("vocab", "fsdp")), P()),
        check_vma=False,
    )
```

profile of v0, /device:TPU:0, one launch (start us, length us, event | category | flops | bytes accessed | tf_op | source)
XLA Modules:
  0.0 130.2 jit_solution(9336433096769030307)
XLA Ops:
  0.6 0.7 convert_element_type.14
  1.3 0.1 convert_element_type.15
  1.4 0.1 broadcast_select_fusion
  1.5 0.7 select_n.15.label_ref
  2.2 1.3 %reshape.55.gain_ref = bf16[1,4096]{1,0:T(2,128)(2,1)} reshape(bf16[4096]{0:T(1024)(128)(2,1)} %param.7) | data formatting | bytes 16384 | tf_op jit(solution)/shard_map/reshape | solution.py:355
  3.5 2.5 %normalize.1.own_ref = bf16[96,4096]{1,0:T(8,128)(2,1)} custom-call(bf16[96,4096]{1,0:T(8,128)(2,1)} %bitcast.5, bf16[1,4096]{1,0:T(2,128)(2,1)} %reshape.55.gain_ref), custom_call_target="tpu_custom_call" | custom-call | tf_op jit(solution)/shard_map/normalize/pallas_call | solution.py:351
  5.9 41.2 %gather_rows.1 = bf16[8,96,4096]{2,1,0:T(8,128)(2,1)} custom-call(bf16[96,4096]{1,0:T(8,128)(2,1)} %normalize.1.own_ref), custom_call_target="tpu_custom_call" | custom-call | tf_op jit(solution)/shard_map/gather_rows/pallas_call | solution.py:130
  47.2 19.6 %local_logits.1 = (f32[768,2048]{1,0:T(8,128)}, f32[4,768]{1,0:T(4,128)}) custom-call(bf16[768,4096]{1,0:T(8,128)(2,1)} %bitcast.3, bf16[4096,2048]{1,0:T(8,128)(2,1)} %weight_ref.3, f32[1,768]{1,0:T(1,128)} %select_n.15.label_ref), custom_call_target="tpu_custom_call" | custom-call | tf_op jit(solution)/shard_map/local_logits/pallas_call | solution.py:264
  66.8 10.7 %exchange_stats.1.stats_ref = f32[4,768]{1,0:T(4,128)} custom-call(f32[4,768]{1,0:T(4,128)} %get-tuple-element.6.x_ref), custom_call_target="tpu_custom_call" | custom-call | tf_op jit(solution)/shard_map/exchange_stats/pallas_call | solution.py:206
  77.4 0.0 copy-start
  77.5 0.0 copy-start.1
  77.5 39.3 %head_update.1 = (f32[4096,2048]{1,0:T(8,128)}, f32[1,4096]{1,0:T(1,128)}) custom-call(bf16[768,4096]{1,0:T(8,128)(2,1)} %bitcast.4, f32[4,768]{1,0:T(4,128)} %exchange_stats.1.stats_ref, f32[768,2048]{1,0:T(8,128)} %get-tuple-element.7.logits_ref, bf16[4096,2048]{1,0:T(8,128)(2,1)} %weight_ref.3, f32[4096,2048]{1,0:T(8,128)} %ema_ref.1), custom_call_target="tpu_custom_call" | custom-call | tf_op jit(solution)/shard_map/head_update/pallas_call | solution.py:325
  116.7 12.1 %exchange_gain.1 = f32[1,4096]{1,0:T(1,128)} custom-call(f32[1,4096]{1,0:T(1,128)} %get-tuple-element.9.x_ref), custom_call_target="tpu_custom_call" | custom-call | tf_op jit(solution)/shard_map/exchange_gain/pallas_call | solution.py:206
  128.8 0.0 copy-done
  128.8 0.0 copy-done.1
  128.8 1.3 %fusion.1 = f32[4096]{0:T(1024)} fusion(f32[4096]{0:T(1024)} %bitcast.6, bf16[4096]{0:T(1024)(128)(2,1)S(1)} %copy-done, f32[4096]{0:T(1024)S(1)} %copy-done.1), kind=kLoop, calls=%fused_computation.2 | loop fusion | flops 28672 | bytes 57344 | tf_op jit(solution)/shard_map/add | solution.py:364
  (1 shorter events, 0.0 us)
Async XLA Ops:
  77.4 51.4 %copy-start = (bf16[4096]{0:T(1024)(128)(2,1)S(1)}, bf16[4096]{0:T(1024)(128)(2,1)}, u32[]{:S(2)}) copy-start(bf16[4096]{0:T(1024)(128)(2,1)} %param.7) | copy-start | bytes 24580
  77.5 51.4 %copy-start.1 = (f32[4096]{0:T(1024)S(1)}, f32[4096]{0:T(1024)}, u32[]{:S(2)}) copy-start(f32[4096]{0:T(1024)} %param.11) | copy-start | bytes 49156
where the time goes:
time: 131 us; the launch traced here: 130 us
  Pallas kernels  125 us (95%)
  other arithmetic  2.1 us (2%)
  local copies, waits for them, and re-layouts  2.08 us (2%)
    pallas_call x1, Pallas kernels, gather_rows(): pl.pallas_call(functools.partial(gather_kernel, parts, ways), out_shape=j...  41.2 us
    pallas_call x1, Pallas kernels, head_update(): pl.pallas_call(functools.partial(update_kernel, chunk), grid=(features //...  39.3 us
    pallas_call x2, Pallas kernels, exchange(): pl.pallas_call(functools.partial(exchange_kernel, parts, ways, combine),...  22.7 us
    pallas_call x1, Pallas kernels, local_logits(): pl.pallas_call(logits_kernel, grid=(columns // tile,), out_shape=(jax.Sha...  19.6 us

commit v1 on v0

v1 whole, which is shorter than its diff:
```python
import functools

import jax
import jax.numpy as jnp
from jax import lax
from jax.experimental import pallas as pl
from jax.experimental.pallas import tpu as pltpu
from jax.sharding import PartitionSpec as P

BETA = 0.99
EPS = 1e-05
LANES = 128
PIECES = 4
LAG = 2
MESH = pl.DeviceIdType.MESH
MIB = 1024 * 1024


def forward_kernel(
    parts,
    ways,
    hidden_ref,
    gain_ref,
    label_ref,
    weight_hbm,
    ema_hbm,
    rows_ref,
    slope_ref,
    early_ref,
    weight_ref,
    hidden_buf,
    logits_ref,
    top_ref,
    total_ref,
    peak_ref,
    label_all,
    label_wide,
    stats_ref,
    half_ref,
    part_slots,
    way_slots,
    load_sem,
    fetch_sem,
    label_send,
    label_recv,
    z_send,
    side_send,
    z_recv,
    y_recv,
    x_recv,
    core_recv,
    stat_send,
    part_recv,
    way_recv,
):
    part, way = lax.axis_index("fsdp"), lax.axis_index("vocab")
    own, features = hidden_ref.shape
    count, columns = logits_ref.shape
    length = parts // 2
    z, y = lax.div(part, 2), lax.rem(part, 2)
    x, core = lax.div(way, 2), lax.rem(way, 2)
    low = jnp.minimum(z, length - 1 - z)
    share = own // 3 // 16 * 16
    wide = own - share
    half = features // 2
    piece = half // PIECES
    block = columns // PIECES
    group = 2 * own

    barrier = pltpu.get_barrier_semaphore()
    for step in range(1, parts):
        pl.semaphore_signal(barrier, inc=1, device_id=(way, lax.rem(part + step, parts)), device_id_type=MESH)
    for step in range(1, ways):
        pl.semaphore_signal(barrier, inc=1, device_id=(lax.rem(way + step, ways), part), device_id_type=MESH)

    load = pltpu.make_async_copy(hidden_ref, hidden_buf, load_sem)
    load.start()
    weight_load = pltpu.make_async_copy(weight_hbm, weight_ref, fetch_sem.at[0])
    weight_load.start()
    early_load = pltpu.make_async_copy(ema_hbm.at[pl.ds(0, early_ref.shape[0]), :], early_ref, fetch_sem.at[1])
    early_load.start()
    top_ref[...] = jnp.full_like(top_ref, -jnp.inf)
    total_ref[...] = jnp.zeros_like(total_ref)
    load.wait()

    @pl.loop(0, own // 16)
    def _(index):
        some = pl.ds(pl.multiple_of(index * 16, 16), 16)
        state = hidden_buf[some, :].astype(jnp.float32)
        factor = lax.rsqrt(jnp.mean(state * state, axis=-1, keepdims=True) + EPS)
        rows_ref[pl.ds(pl.multiple_of(part * own + index * 16, 16), 16), :] = (
            state * factor * gain_ref[...].astype(jnp.float32)
        ).astype(jnp.bfloat16)

    pl.semaphore_wait(barrier, parts + ways - 2)

    def source(step):
        both = (step <= 2 * low).astype(jnp.int32)
        left = both * lax.rem(step, 2) + (1 - both) * (2 * z > length - 1).astype(jnp.int32)
        far = both * lax.div(step + 1, 2) + (1 - both) * (step - low)
        return z + far - 2 * far * left, left

    def view(index, start, size, side, s):
        return rows_ref.at[
            pl.ds(pl.multiple_of(index * own + start, 16), size),
            pl.ds(pl.multiple_of(side * half + s * piece, LANES), piece),
        ]

    def send(target, send_sem, recv_sem, device):
        pltpu.make_async_remote_copy(
            src_ref=target, dst_ref=target, send_sem=send_sem, recv_sem=recv_sem, device_id=device, device_id_type=MESH
        ).start()

    across_y = (way, 2 * z + 1 - y)
    across_x = (2 * (1 - x) + core, part)
    across_core = (2 * x + 1 - core, part)

    def arrive(target, recv_sem):
        pltpu.make_async_remote_copy(
            src_ref=target, dst_ref=target, send_sem=side_send.at[0], recv_sem=recv_sem, device_id=across_y, device_id_type=MESH
        ).wait_recv()

    def sent(target, send_sem):
        pltpu.make_async_remote_copy(
            src_ref=target, dst_ref=target, send_sem=send_sem, recv_sem=core_recv.at[0], device_id=across_y, device_id_type=MESH
        ).wait_send()

    def send_z(index, target_z, s, slot):
        where = view(2 * index + y, x * share, wide, core, s)
        send(where, z_send.at[slot], z_recv.at[index, s], (way, 2 * target_z + y))

    def send_y(step, index, s):
        send(view(2 * index + y, x * share, wide, core, s), side_send.at[0], y_recv.at[step, s], across_y)

    def send_x(index, s):
        if share:
            send(view(index, x * wide, share, core, s), side_send.at[1], x_recv.at[index, s], across_x)

    def send_core(index, step, start, size, s):
        send(view(index, start, size, core, s), side_send.at[2], core_recv.at[step], across_core)

    for s in range(PIECES):
        send_y(0, z, s)

        @pl.when(z > 0)
        def _():
            send_z(z, z - 1, s, 0)

        @pl.when(z < length - 1)
        def _():
            send_z(z, z + 1, s, 1)

    labels = []
    for step in range(1, parts):
        labels.append(
            pltpu.make_async_remote_copy(
                src_ref=label_ref,
                dst_ref=label_all.at[part],
                send_sem=label_send.at[step - 1],
                recv_sem=label_recv.at[step - 1],
                device_id=(way, lax.rem(part + step, parts)),
                device_id_type=MESH,
            )
        )
        labels[-1].start()
    label_all[part] = label_ref[...]
    weight_load.wait()

    def group_source(step):
        first = (step == 0).astype(jnp.int32)
        return first * z + (1 - first) * source(step)[0]

    @pl.loop(0, length * PIECES + PIECES + LAG)
    def _(q):
        step, s = lax.div(q, PIECES), lax.rem(q, PIECES)

        @pl.when(q < length * PIECES)
        def _():
            index = 2 * group_source(step) + 1 - y
            arrive(view(index, x * share, wide, core, s), y_recv.at[step, s])
            send_x(index, s)
            send_core(index, step, x * share, wide, s)

        @pl.when(q < (length - 1) * PIECES)
        def _():
            origin, left = source(step + 1)
            onward = z - 1 + 2 * left
            index = 2 * origin + y
            arrive(view(index, x * share, wide, core, s), z_recv.at[origin, s])

            @pl.when(jnp.logical_and(onward >= 0, onward < length))
            def _():
                send_z(origin, onward, s, step + 2)

            send_y(step + 1, origin, s)
            send_x(index, s)
            send_core(index, step + 1, x * share, wide, s)

        if share:
            late = q - LAG
            late_step, late_s = lax.div(late, PIECES), lax.rem(late, PIECES)

            @pl.when(jnp.logical_and(late >= 0, late < length * PIECES))
            def _():
                index = 2 * group_source(late_step) + 1 - y
                arrive(view(index, (1 - x) * wide, share, core, late_s), x_recv.at[index, late_s])
                send_core(index, late_step, (1 - x) * wide, share, late_s)

            @pl.when(jnp.logical_and(late >= 0, late < (length - 1) * PIECES))
            def _():
                index = 2 * source(late_step + 1)[0] + y
                arrive(view(index, (1 - x) * wide, share, core, late_s), x_recv.at[index, late_s])
                send_core(index, late_step + 1, (1 - x) * wide, share, late_s)

        ready = q - PIECES - LAG
        turn, n = lax.div(ready, PIECES), lax.rem(ready, PIECES)

        @pl.when(ready >= 0)
        def _():
            origin = group_source(turn)

            @pl.when(ready == 0)
            def _():
                arrive(rows_ref.at[pl.ds(0, own), pl.ds(0, half)], core_recv.at[0])

            @pl.when(jnp.logical_and(ready > 0, n == 0))
            def _():
                arrive(rows_ref.at[pl.ds(0, group), pl.ds(0, half)], core_recv.at[turn])

            some = pl.ds(pl.multiple_of(origin * group, 16), group)
            result = jnp.dot(
                rows_ref[some, :],
                weight_ref[:, pl.ds(pl.multiple_of(n * block, LANES), block)],
                preferred_element_type=jnp.float32,
            )
            logits_ref[some, pl.ds(pl.multiple_of(n * block, LANES), block)] = result
            pieces = [result[:, start : start + LANES] for start in range(0, block, LANES)]
            old = top_ref[some, :]
            top = functools.reduce(jnp.maximum, pieces, old)
            total_ref[some, :] = total_ref[some, :] * jnp.exp(old - top) + sum(jnp.exp(item - top) for item in pieces)
            top_ref[some, :] = top

    wide_top = top_ref[...].T
    row_top = jnp.max(wide_top, axis=0, keepdims=True)
    row_total = jnp.sum(total_ref[...].T * jnp.exp(wide_top - row_top), axis=0, keepdims=True)
    stats_ref[...] = jnp.concatenate([row_top, row_total], axis=0)

    def combine(terms):
        top = functools.reduce(jnp.maximum, [term[0:1] for term in terms])
        total = sum(term[1:2] * jnp.exp(term[0:1] - top) for term in terms)
        return jnp.concatenate([top, total], axis=0)

    copies = []
    for step in range(1, parts):
        copies.append(
            pltpu.make_async_remote_copy(
                src_ref=stats_ref,
                dst_ref=part_slots.at[part],
                send_sem=stat_send.at[step - 1],
                recv_sem=part_recv.at[step - 1],
                device_id=(way, lax.rem(part + step, parts)),
                device_id_type=MESH,
            )
        )
        copies[-1].start()
    part_slots[part] = stats_ref[...]

    for step in range(1, parts):
        pltpu.make_async_remote_copy(
            src_ref=label_ref,
            dst_ref=label_all.at[lax.rem(part + parts - step, parts)],
            send_sem=label_send.at[step - 1],
            recv_sem=label_recv.at[step - 1],
            device_id=(way, lax.rem(part + step, parts)),
            device_id_type=MESH,
        ).wait_recv()

    @pl.loop(0, parts)
    def _(index):
        some = pl.ds(pl.multiple_of(index * own, 16), own)
        peak = jnp.broadcast_to(jnp.max(top_ref[some, :], axis=1, keepdims=True), (own, LANES))
        first = (way * parts + part) * columns
        label_wide[some, :] = jnp.broadcast_to(label_all[index].astype(jnp.float32), (LANES, own)).T.astype(jnp.int32) - first
        for start in range(0, columns, LANES):
            logits_ref[some, start : start + LANES] = jnp.exp(logits_ref[some, start : start + LANES] - peak)

    for step in range(1, parts):
        pltpu.make_async_remote_copy(
            src_ref=stats_ref,
            dst_ref=part_slots.at[lax.rem(part + parts - step, parts)],
            send_sem=stat_send.at[step - 1],
            recv_sem=part_recv.at[step - 1],
            device_id=(way, lax.rem(part + step, parts)),
            device_id_type=MESH,
        ).wait_recv()
    half_ref[...] = combine([part_slots[index] for index in range(parts)])
    for step in range(1, ways):
        copies.append(
            pltpu.make_async_remote_copy(
                src_ref=half_ref,
                dst_ref=way_slots.at[way],
                send_sem=stat_send.at[parts - 2 + step],
                recv_sem=way_recv.at[step - 1],
                device_id=(lax.rem(way + step, ways), part),
                device_id_type=MESH,
            )
        )
        copies[-1].start()
    way_slots[way] = half_ref[...]
    for step in range(1, ways):
        pltpu.make_async_remote_copy(
            src_ref=half_ref,
            dst_ref=way_slots.at[lax.rem(way + ways - step, ways)],
            send_sem=stat_send.at[parts - 2 + step],
            recv_sem=way_recv.at[step - 1],
            device_id=(lax.rem(way + step, ways), part),
            device_id_type=MESH,
        ).wait_recv()
    final = combine([way_slots[index] for index in range(ways)])
    coefficient = jnp.exp(stats_ref[0:1] - final[0:1]) / final[1:2]
    peak_ref[...] = jnp.broadcast_to(coefficient, (LANES, count)).T

    @pl.loop(0, parts)
    def _(index):
        some = pl.ds(pl.multiple_of(index * own, 16), own)
        scale, label = peak_ref[some, :], label_wide[some, :]
        lane = lax.broadcasted_iota(jnp.int32, (own, LANES), 1)
        for start in range(0, columns, LANES):
            chances = logits_ref[some, start : start + LANES] * scale
            hits = (label == lane + start).astype(jnp.float32)
            slope_ref[some, start : start + LANES] = (chances - hits).astype(slope_ref.dtype)

    for copy in labels + copies:
        copy.wait_send()
    sent(rows_ref.at[pl.ds(0, length * wide), pl.ds(0, half)], side_send.at[0])
    if share:
        sent(rows_ref.at[pl.ds(0, (parts - 1) * share), pl.ds(0, half)], side_send.at[1])
    sent(rows_ref.at[pl.ds(0, (parts - 1) * own), pl.ds(0, half)], side_send.at[2])
    part_view = rows_ref.at[pl.ds(0, wide), pl.ds(0, half)]

    @pl.when(z > 0)
    def _():
        sent(part_view, z_send.at[0])

    @pl.when(z < length - 1)
    def _():
        sent(part_view, z_send.at[1])

    for step in range(1, length):
        onward = z - 1 + 2 * source(step)[1]

        @pl.when(jnp.logical_and(onward >= 0, onward < length))
        def _():
            sent(part_view, z_send.at[step + 1])

    early_load.wait()


def forward(hidden, gain, labels, head_weight, head_ema, parts, ways, early, limit):
    own, features = hidden.shape
    columns = head_weight.shape[1]
    count = own * parts
    length = parts // 2
    anywhere = pl.BlockSpec(memory_space=pl.ANY)
    near = pl.BlockSpec(memory_space=pltpu.VMEM)
    dma = pltpu.SemaphoreType.DMA
    wide = pltpu.VMEM((count, LANES), jnp.float32)
    return pl.pallas_call(
        functools.partial(forward_kernel, parts, ways),
        out_shape=(
            pltpu.VMEM((count, features), jnp.bfloat16),
            pltpu.VMEM((count, columns), jnp.bfloat16),
            pltpu.VMEM((early, columns), jnp.float32),
        ),
        in_specs=[anywhere, near, near, anywhere, anywhere],
        out_specs=(near,) * 3,
        scratch_shapes=[
            pltpu.VMEM((features, columns), jnp.bfloat16),
            pltpu.VMEM((own, features), jnp.bfloat16),
            pltpu.VMEM((count, columns), jnp.float32),
            wide,
            wide,
            wide,
            pltpu.VMEM((parts, 1, own), jnp.int32),
            pltpu.VMEM((count, LANES), jnp.int32),
            pltpu.VMEM((2, count), jnp.float32),
            pltpu.VMEM((2, count), jnp.float32),
            pltpu.VMEM((parts, 2, count), jnp.float32),
            pltpu.VMEM((ways, 2, count), jnp.float32),
            dma,
            dma((2,)),
            dma((parts - 1,)),
            dma((parts - 1,)),
            dma((length + 1,)),
            dma((3,)),
            dma((length, PIECES)),
            dma((length, PIECES)),
            dma((parts, PIECES)),
            dma((length,)),
            dma((parts + ways - 2,)),
            dma((parts - 1,)),
            dma((ways - 1,)),
        ],
        compiler_params=pltpu.CompilerParams(collective_id=0, has_side_effects=True, vmem_limit_bytes=limit),
        name="forward",
    )(hidden, gain, labels, head_weight, head_ema)


def update_kernel(
    tile,
    close,
    rows_ref,
    slope_ref,
    early_ref,
    weight_hbm,
    ema_hbm,
    new_hbm,
    gain_ref,
    rows_buf,
    weight_buf,
    ema_buf,
    new_buf,
    rows_sem,
    weight_sem,
    in_sem,
    out_sem,
):
    count, columns = slope_ref.shape
    features = rows_ref.shape[1]
    tiles, early = features // tile, early_ref.shape[0] // tile
    mix = (1.0 - BETA) / count
    width = min(512, columns)

    def rows_of(index):
        return pl.ds(pl.multiple_of(index * tile, tile), tile)

    def fetch(index):
        slot = lax.rem(index, 2)
        return pltpu.make_async_copy(ema_hbm.at[rows_of(index), :], ema_buf.at[slot], in_sem.at[slot])

    def fetch_rows(index):
        slot = lax.rem(index, 2)
        return pltpu.make_async_copy(rows_ref.at[:, rows_of(index)], rows_buf.at[slot], rows_sem.at[slot])

    def fetch_weight(index):
        slot = lax.rem(index, 2)
        return pltpu.make_async_copy(weight_hbm.at[rows_of(index), :], weight_buf.at[slot], weight_sem.at[slot])

    def store(index):
        slot = lax.rem(index, 2)
        return pltpu.make_async_copy(new_buf.at[slot], new_hbm.at[rows_of(index), :], out_sem.at[slot])

    def work(index, old):
        slot = lax.rem(index, 2)

        @pl.when(index >= 2)
        def _():
            store(index - 2).wait()

        fetch_weight(index).wait()
        if close:
            tall = rows_ref[:, rows_of(index)].T
        else:
            fetch_rows(index).wait()
            tall = rows_buf[slot].T
        total = jnp.zeros((tile, LANES), jnp.float32)
        for start in range(0, columns, width):
            gradient = jnp.dot(tall, slope_ref[:, start : start + width], preferred_element_type=jnp.float32)
            new_buf[slot, :, start : start + width] = BETA * old(start) + mix * gradient * gradient
            product = weight_buf[slot, :, start : start + width].astype(jnp.float32) * gradient
            for lane in range(0, width, LANES):
                total = total + product[:, lane : lane + LANES]
        gain_ref[:, rows_of(index)] = jnp.sum(total.T, axis=0, keepdims=True)
        store(index).start()

        @pl.when(index + 2 < tiles)
        def _():
            fetch_weight(index + 2).start()
            if not close:
                fetch_rows(index + 2).start()

    for index in range(min(2, tiles)):
        fetch_weight(index).start()
        if not close:
            fetch_rows(index).start()
    for index in range(early, min(early + 2, tiles)):
        fetch(index).start()

    @pl.loop(0, early)
    def _(index):
        work(index, lambda start: early_ref[rows_of(index), start : start + width])

    @pl.loop(early, tiles)
    def _(index):
        fetch(index).wait()
        work(index, lambda start: ema_buf[lax.rem(index, 2), :, start : start + width])

        @pl.when(index + 2 < tiles)
        def _():
            fetch(index + 2).start()

    for index in range(max(tiles - 2, 0), tiles):
        store(index).wait()


def head_update(rows, slope, early, head_weight, head_ema, tile, close, limit):
    features, columns = head_ema.shape
    anywhere = pl.BlockSpec(memory_space=pl.ANY)
    near = pl.BlockSpec(memory_space=pltpu.VMEM)
    dma = pltpu.SemaphoreType.DMA
    return pl.pallas_call(
        functools.partial(update_kernel, tile, close),
        out_shape=(
            jax.ShapeDtypeStruct((features, columns), jnp.float32),
            jax.ShapeDtypeStruct((1, features), jnp.float32),
        ),
        in_specs=[near if close else anywhere, near, near, anywhere, anywhere],
        out_specs=(anywhere, near),
        scratch_shapes=[
            pltpu.VMEM((2, 16, LANES) if close else (2, rows.shape[0], tile), jnp.bfloat16),
            pltpu.VMEM((2, tile, columns), jnp.bfloat16),
            pltpu.VMEM((2, tile, columns), jnp.float32),
            pltpu.VMEM((2, tile, columns), jnp.float32),
        ]
        + [dma((2,))] * 4,
        compiler_params=pltpu.CompilerParams(vmem_limit_bytes=limit),
        name="head_update",
    )(rows, slope, early, head_weight, head_ema)


def exchange_kernel(parts, ways, x_ref, y_ref, part_slots, way_slots, half, send_sem, part_sem, way_sem):
    part, way = lax.axis_index("fsdp"), lax.axis_index("vocab")
    barrier = pltpu.get_barrier_semaphore()
    for step in range(1, parts):
        pl.semaphore_signal(barrier, inc=1, device_id=(way, lax.rem(part + step, parts)), device_id_type=MESH)
    for step in range(1, ways):
        pl.semaphore_signal(barrier, inc=1, device_id=(lax.rem(way + step, ways), part), device_id_type=MESH)
    pl.semaphore_wait(barrier, parts + ways - 2)

    copies = []
    for step in range(1, parts):
        copies.append(
            pltpu.make_async_remote_copy(
                src_ref=x_ref,
                dst_ref=part_slots.at[part],
                send_sem=send_sem.at[step - 1],
                recv_sem=part_sem.at[step - 1],
                device_id=(way, lax.rem(part + step, parts)),
                device_id_type=MESH,
            )
        )
        copies[-1].start()
    part_slots[part] = x_ref[...]
    for step in range(1, parts):
        pltpu.make_async_remote_copy(
            src_ref=x_ref,
            dst_ref=part_slots.at[lax.rem(part + parts - step, parts)],
            send_sem=send_sem.at[step - 1],
            recv_sem=part_sem.at[step - 1],
            device_id=(way, lax.rem(part + step, parts)),
            device_id_type=MESH,
        ).wait_recv()
    half[...] = sum(part_slots[index] for index in range(parts))
    for step in range(1, ways):
        copies.append(
            pltpu.make_async_remote_copy(
                src_ref=half,
                dst_ref=way_slots.at[way],
                send_sem=send_sem.at[parts - 2 + step],
                recv_sem=way_sem.at[step - 1],
                device_id=(lax.rem(way + step, ways), part),
                device_id_type=MESH,
            )
        )
        copies[-1].start()
    way_slots[way] = half[...]
    for step in range(1, ways):
        pltpu.make_async_remote_copy(
            src_ref=half,
            dst_ref=way_slots.at[lax.rem(way + ways - step, ways)],
            send_sem=send_sem.at[parts - 2 + step],
            recv_sem=way_sem.at[step - 1],
            device_id=(lax.rem(way + step, ways), part),
            device_id_type=MESH,
        ).wait_recv()
    y_ref[...] = sum(way_slots[index] for index in range(ways))
    for copy in copies:
        copy.wait_send()


def exchange(x, parts, ways):
    return pl.pallas_call(
        functools.partial(exchange_kernel, parts, ways),
        out_shape=jax.ShapeDtypeStruct(x.shape, x.dtype),
        in_specs=[pl.BlockSpec(memory_space=pltpu.VMEM)],
        out_specs=pl.BlockSpec(memory_space=pltpu.VMEM),
        scratch_shapes=[
            pltpu.VMEM((parts,) + x.shape, x.dtype),
            pltpu.VMEM((ways,) + x.shape, x.dtype),
            pltpu.VMEM(x.shape, x.dtype),
            pltpu.SemaphoreType.DMA((parts + ways - 2,)),
            pltpu.SemaphoreType.DMA((parts - 1,)),
            pltpu.SemaphoreType.DMA((ways - 1,)),
        ],
        compiler_params=pltpu.CompilerParams(collective_id=1, has_side_effects=True, vmem_limit_bytes=8 * MIB),
        name="exchange_gain",
    )(x)


def on_device(parts, ways, hidden, norm_gain, labels, head_weight, head_ema, gain_ema):
    batches, own_rows, features = hidden.shape
    own = batches * own_rows
    count = own * parts
    columns = head_weight.shape[1]
    tile = 512 if features % 512 == 0 else 256
    slab = tile * columns * 4
    close = count * features * 2 <= 12 * MIB
    limit = max(features * columns * 2 + count * (columns + 4 * LANES) * 4, 5 * slab) + 4 * MIB
    room = 52 * MIB - limit - count * (features + columns) * 2
    early = min(max(room // slab, 1), features // tile) * tile
    rows, slope, early_ema = forward(
        hidden.reshape(own, features), norm_gain.reshape(1, features), labels.reshape(1, own), head_weight, head_ema, parts, ways, early, limit
    )
    head_new, partial_sum = head_update(rows, slope, early_ema, head_weight, head_ema, tile, close, limit)
    gain_grad = exchange(partial_sum, parts, ways).reshape(features) / norm_gain.astype(jnp.float32)
    gain_new = BETA * gain_ema + (1.0 - BETA) * gain_grad * gain_grad / count
    return (head_new, gain_new)


def solution(mesh):
    return jax.shard_map(
        functools.partial(on_device, mesh.shape["fsdp"], mesh.shape["vocab"]),
        mesh=mesh,
        in_specs=(
            P(None, "fsdp", None),
            P(),
            P(None, "fsdp"),
            P(None, ("vocab", "fsdp")),
            P(None, ("vocab", "fsdp")),
            P(),
        ),
        out_specs=(P(None, ("vocab", "fsdp")), P()),
        check_vma=False,
    )
```

time: 131 us -> 97.5 us (0.74)
  Pallas kernels: 125 us -> 93.3 us
  other arithmetic: 2.1 us -> 0.62 us
    pallas_call x6 -> x3, Pallas kernels: 125 us -> 93.3 us  [the longest x1 54.1 us: forward(): pl.pallas_call(functools.partial(forward_kernel, parts, ways), out_shape=...]
where the time goes in v1:
time: 97.5 us; the launch traced here: 97.2 us
  Pallas kernels  93.3 us (96%)
  local copies, waits for them, and re-layouts  2.61 us (3%)
    pallas_call x1, Pallas kernels, forward(): pl.pallas_call(functools.partial(forward_kernel, parts, ways), out_shape=...  54.1 us
    pallas_call x1, Pallas kernels, head_update(): pl.pallas_call(functools.partial(update_kernel, tile, close), out_shape=(...  29.4 us
    pallas_call x1, Pallas kernels, exchange(): pl.pallas_call(functools.partial(exchange_kernel, parts, ways), out_shape...  9.85 us

profile of v1, /device:TPU:0, one launch (start us, length us, event | category | flops | bytes accessed | tf_op | source)
XLA Modules:
  0.0 97.2 jit_solution(9009936491404089859)
XLA Ops:
  0.6 0.8 reshape.18.label_ref
  1.4 0.7 reshape.17.gain_ref
  2.1 0.0 copy-start
  2.1 1.1 %copy-done = bf16[2,48,4096]{2,1,0:T(8,128)(2,1)S(1)} copy-done((bf16[2,48,4096]{2,1,0:T(8,128)(2,1)S(1)}, bf16[2,48,4096]{2,1,0:T(8,128)(2,1)}, u32[]{:S(2)}) %copy-start) | copy-done | bytes 786456
  3.2 54.1 %forward.1 = (bf16[768,4096]{1,0:T(8,128)(2,1)S(1)}, bf16[768,2048]{1,0:T(8,128)(2,1)S(1)}, f32[1536,2048]{1,0:T(8,128)S(1)}) custom-call(bf16[96,4096]{1,0:T(8,128)(2,1)S(1)} %bitcast.2, bf16[1,4096]{1,0:T(2,128)(2,1)S(1)} %reshape.17.gain_ref, s32[1,96]{1,0:T(1,128)S(1)} %reshape.18.label_ref, bf16[4096,2048]{1,0:T(8,128)(2,1)} %weight_hbm.3, ...), custom_call_target="tpu_custom_call" | custom-call | tf_op jit(solution)/shard_map/forward/pallas_call | solution.py:368
  57.3 0.0 copy-start.1
  57.3 0.0 copy-start.2
  57.3 29.4 %head_update.1 = (f32[4096,2048]{1,0:T(8,128)}, f32[1,4096]{1,0:T(1,128)S(1)}) custom-call(bf16[768,4096]{1,0:T(8,128)(2,1)S(1)} %get-tuple-element.7.rows_ref, bf16[768,2048]{1,0:T(8,128)(2,1)S(1)} %get-tuple-element.8.slope_ref, f32[1536,2048]{1,0:T(8,128)S(1)} %get-tuple-element.9.early_ref, bf16[4096,2048]{1,0:T(8,128)(2,1)} %weight_hbm.3, ...), custom_call_target="tpu_custom_call" | custom-call | tf_op jit(solution)/shard_map/head_update/pallas_call | solution.py:511
  86.7 9.9 %exchange_gain.1 = f32[1,4096]{1,0:T(1,128)S(1)} custom-call(f32[1,4096]{1,0:T(1,128)S(1)} %get-tuple-element.11.x_ref), custom_call_target="tpu_custom_call" | custom-call | tf_op jit(solution)/shard_map/exchange_gain/pallas_call | solution.py:592
  96.6 0.0 copy-done.1
  96.6 0.0 copy-done.2
  96.6 0.6 fusion.1
Async XLA Ops:
  2.1 1.1 %copy-start = (bf16[2,48,4096]{2,1,0:T(8,128)(2,1)S(1)}, bf16[2,48,4096]{2,1,0:T(8,128)(2,1)}, u32[]{:S(2)}) copy-start(bf16[2,48,4096]{2,1,0:T(8,128)(2,1)} %param.6) | copy-start | bytes 2359300
  57.3 39.3 %copy-start.1 = (bf16[4096]{0:T(1024)(128)(2,1)S(1)}, bf16[4096]{0:T(1024)(128)(2,1)}, u32[]{:S(2)}) copy-start(bf16[4096]{0:T(1024)(128)(2,1)} %param.7) | copy-start | bytes 24580
  57.3 39.3 %copy-start.2 = (f32[4096]{0:T(1024)S(1)}, f32[4096]{0:T(1024)}, u32[]{:S(2)}) copy-start(f32[4096]{0:T(1024)} %param.11) | copy-start | bytes 49156

commit v2 on v1

--- a/solution.py
+++ b/solution.py
@@ -11,12 +11,31 @@
 EPS = 1e-05
 LANES = 128
 PIECES = 4
-LAG = 2
+LAG = 3
 MESH = pl.DeviceIdType.MESH
 MIB = 1024 * 1024
 
 
 def forward_kernel(
+    parts,
+    ways,
+    early,
+    hidden_ref,
+    gain_ref,
+    label_ref,
+    weight_hbm,
+    ema_hbm,
+    *refs,
+):
+    rows_ref, slope_ref = refs[:2]
+    weight_refs, early_refs = refs[2 : 2 + PIECES], refs[2 + PIECES : 2 + PIECES + early]
+    scratch = refs[2 + PIECES + early :]
+    forward_body(
+        parts, ways, hidden_ref, gain_ref, label_ref, weight_hbm, ema_hbm, rows_ref, slope_ref, weight_refs, early_refs, *scratch
+    )
+
+
+def forward_body(
     parts,
     ways,
     hidden_ref,
@@ -26,9 +45,8 @@
     ema_hbm,
     rows_ref,
     slope_ref,
-    early_ref,
-    weight_ref,
-    hidden_buf,
+    weight_refs,
+    early_refs,
     logits_ref,
     top_ref,
     total_ref,
@@ -39,7 +57,6 @@
     half_ref,
     part_slots,
     way_slots,
-    load_sem,
     fetch_sem,
     label_send,
     label_recv,
@@ -73,20 +90,20 @@
     for step in range(1, ways):
         pl.semaphore_signal(barrier, inc=1, device_id=(lax.rem(way + step, ways), part), device_id_type=MESH)
 
-    load = pltpu.make_async_copy(hidden_ref, hidden_buf, load_sem)
-    load.start()
-    weight_load = pltpu.make_async_copy(weight_hbm, weight_ref, fetch_sem.at[0])
-    weight_load.start()
-    early_load = pltpu.make_async_copy(ema_hbm.at[pl.ds(0, early_ref.shape[0]), :], early_ref, fetch_sem.at[1])
-    early_load.start()
+    loads = []
+    for n, ref in enumerate(weight_refs):
+        loads.append(pltpu.make_async_copy(weight_hbm.at[:, pl.ds(n * block, block)], ref, fetch_sem.at[n]))
+    for n, ref in enumerate(early_refs):
+        loads.append(pltpu.make_async_copy(ema_hbm.at[pl.ds(n * ref.shape[0], ref.shape[0]), :], ref, fetch_sem.at[PIECES + n]))
+    for load in loads:
+        load.start()
     top_ref[...] = jnp.full_like(top_ref, -jnp.inf)
     total_ref[...] = jnp.zeros_like(total_ref)
-    load.wait()
 
     @pl.loop(0, own // 16)
     def _(index):
         some = pl.ds(pl.multiple_of(index * 16, 16), 16)
-        state = hidden_buf[some, :].astype(jnp.float32)
+        state = hidden_ref[some, :].astype(jnp.float32)
         factor = lax.rsqrt(jnp.mean(state * state, axis=-1, keepdims=True) + EPS)
         rows_ref[pl.ds(pl.multiple_of(part * own + index * 16, 16), 16), :] = (
             state * factor * gain_ref[...].astype(jnp.float32)
@@ -164,7 +181,8 @@
         )
         labels[-1].start()
     label_all[part] = label_ref[...]
-    weight_load.wait()
+    for load in loads[:PIECES]:
+        load.wait()
 
     def group_source(step):
         first = (step == 0).astype(jnp.int32)
@@ -228,17 +246,17 @@
                 arrive(rows_ref.at[pl.ds(0, group), pl.ds(0, half)], core_recv.at[turn])
 
             some = pl.ds(pl.multiple_of(origin * group, 16), group)
-            result = jnp.dot(
-                rows_ref[some, :],
-                weight_ref[:, pl.ds(pl.multiple_of(n * block, LANES), block)],
-                preferred_element_type=jnp.float32,
-            )
-            logits_ref[some, pl.ds(pl.multiple_of(n * block, LANES), block)] = result
-            pieces = [result[:, start : start + LANES] for start in range(0, block, LANES)]
-            old = top_ref[some, :]
-            top = functools.reduce(jnp.maximum, pieces, old)
-            total_ref[some, :] = total_ref[some, :] * jnp.exp(old - top) + sum(jnp.exp(item - top) for item in pieces)
-            top_ref[some, :] = top
+            for which, weight_ref in enumerate(weight_refs):
+
+                @pl.when(n == which)
+                def _():
+                    result = jnp.dot(rows_ref[some, :], weight_ref[...], preferred_element_type=jnp.float32)
+                    logits_ref[some, which * block : (which + 1) * block] = result
+                    pieces = [result[:, start : start + LANES] for start in range(0, block, LANES)]
+                    old = top_ref[some, :]
+                    top = functools.reduce(jnp.maximum, pieces, old)
+                    total_ref[some, :] = total_ref[some, :] * jnp.exp(old - top) + sum(jnp.exp(item - top) for item in pieces)
+                    top_ref[some, :] = top
 
     wide_top = top_ref[...].T
     row_top = jnp.max(wide_top, axis=0, keepdims=True)
@@ -280,7 +298,10 @@
         some = pl.ds(pl.multiple_of(index * own, 16), own)
         peak = jnp.broadcast_to(jnp.max(top_ref[some, :], axis=1, keepdims=True), (own, LANES))
         first = (way * parts + part) * columns
-        label_wide[some, :] = jnp.broadcast_to(label_all[index].astype(jnp.float32), (LANES, own)).T.astype(jnp.int32) - first
+        for batch, line in enumerate(range(0, own, label_ref.shape[1])):
+            row = label_all[index, batch : batch + 1].astype(jnp.float32)
+            wide_row = jnp.broadcast_to(row, (LANES, label_ref.shape[1])).T.astype(jnp.int32) - first
+            label_wide[pl.ds(pl.multiple_of(index * own + line, 16), label_ref.shape[1]), :] = wide_row
         for start in range(0, columns, LANES):
             logits_ref[some, start : start + LANES] = jnp.exp(logits_ref[some, start : start + LANES] - peak)
 
@@ -353,10 +374,11 @@
         def _():
             sent(part_view, z_send.at[step + 1])
 
-    early_load.wait()
-
-
-def forward(hidden, gain, labels, head_weight, head_ema, parts, ways, early, limit):
+    for load in loads[PIECES:]:
+        load.wait()
+
+
+def forward(hidden, gain, labels, head_weight, head_ema, parts, ways, early, tile, limit):
     own, features = hidden.shape
     columns = head_weight.shape[1]
     count = own * parts
@@ -366,29 +388,27 @@
     dma = pltpu.SemaphoreType.DMA
     wide = pltpu.VMEM((count, LANES), jnp.float32)
     return pl.pallas_call(
-        functools.partial(forward_kernel, parts, ways),
+        functools.partial(forward_kernel, parts, ways, early),
         out_shape=(
             pltpu.VMEM((count, features), jnp.bfloat16),
             pltpu.VMEM((count, columns), jnp.bfloat16),
-            pltpu.VMEM((early, columns), jnp.float32),
-        ),
-        in_specs=[anywhere, near, near, anywhere, anywhere],
-        out_specs=(near,) * 3,
+        )
+        + (pltpu.VMEM((features, columns // PIECES), jnp.bfloat16),) * PIECES
+        + (pltpu.VMEM((tile, columns), jnp.float32),) * early,
+        in_specs=[near, near, near, anywhere, anywhere],
+        out_specs=(near,) * (2 + PIECES + early),
         scratch_shapes=[
-            pltpu.VMEM((features, columns), jnp.bfloat16),
-            pltpu.VMEM((own, features), jnp.bfloat16),
             pltpu.VMEM((count, columns), jnp.float32),
             wide,
             wide,
             wide,
-            pltpu.VMEM((parts, 1, own), jnp.int32),
+            pltpu.VMEM((parts,) + labels.shape, jnp.int32),
             pltpu.VMEM((count, LANES), jnp.int32),
             pltpu.VMEM((2, count), jnp.float32),
             pltpu.VMEM((2, count), jnp.float32),
             pltpu.VMEM((parts, 2, count), jnp.float32),
             pltpu.VMEM((ways, 2, count), jnp.float32),
-            dma,
-            dma((2,)),
+            dma((PIECES + early,)),
             dma((parts - 1,)),
             dma((parts - 1,)),
             dma((length + 1,)),
@@ -406,126 +426,88 @@
     )(hidden, gain, labels, head_weight, head_ema)
 
 
-def update_kernel(
-    tile,
-    close,
-    rows_ref,
-    slope_ref,
-    early_ref,
-    weight_hbm,
-    ema_hbm,
-    new_hbm,
-    gain_ref,
-    rows_buf,
-    weight_buf,
-    ema_buf,
-    new_buf,
-    rows_sem,
-    weight_sem,
-    in_sem,
-    out_sem,
-):
+def update_kernel(tile, close, early, ema_hbm, rows_ref, slope_ref, *refs):
+    weight_refs, early_refs = refs[:PIECES], refs[PIECES : PIECES + early]
+    new_hbm, gain_ref, rows_buf, slab, rows_sem, in_sem, out_sem = refs[PIECES + early :]
     count, columns = slope_ref.shape
-    features = rows_ref.shape[1]
-    tiles, early = features // tile, early_ref.shape[0] // tile
+    tiles = gain_ref.shape[1] // tile
+    depth = slab.shape[0]
     mix = (1.0 - BETA) / count
-    width = min(512, columns)
-
-    def rows_of(index):
-        return pl.ds(pl.multiple_of(index * tile, tile), tile)
-
-    def fetch(index):
-        slot = lax.rem(index, 2)
-        return pltpu.make_async_copy(ema_hbm.at[rows_of(index), :], ema_buf.at[slot], in_sem.at[slot])
-
-    def fetch_rows(index):
-        slot = lax.rem(index, 2)
-        return pltpu.make_async_copy(rows_ref.at[:, rows_of(index)], rows_buf.at[slot], rows_sem.at[slot])
-
-    def fetch_weight(index):
-        slot = lax.rem(index, 2)
-        return pltpu.make_async_copy(weight_hbm.at[rows_of(index), :], weight_buf.at[slot], weight_sem.at[slot])
-
-    def store(index):
-        slot = lax.rem(index, 2)
-        return pltpu.make_async_copy(new_buf.at[slot], new_hbm.at[rows_of(index), :], out_sem.at[slot])
-
-    def work(index, old):
-        slot = lax.rem(index, 2)
-
-        @pl.when(index >= 2)
-        def _():
-            store(index - 2).wait()
-
-        fetch_weight(index).wait()
+    width = columns // PIECES
+    late = list(range(early, tiles))
+    order = []
+    for index in range(early):
+        order += [index] + late[:1]
+        late = late[1:]
+    order += late
+
+    def fetch(place):
+        slot = place % depth
+        return pltpu.make_async_copy(ema_hbm.at[pl.ds(order[place] * tile, tile), :], slab.at[slot], in_sem.at[slot])
+
+    def fetch_rows(place):
+        return pltpu.make_async_copy(rows_ref.at[:, pl.ds(order[place] * tile, tile)], rows_buf, rows_sem)
+
+    def store(place, start, size):
+        slot = place % depth
+        return pltpu.make_async_copy(
+            slab.at[slot, :, pl.ds(start, size)], new_hbm.at[pl.ds(order[place] * tile, tile), pl.ds(start, size)], out_sem.at[slot]
+        )
+
+    if order[0] >= early:
+        fetch(0).start()
+    for place, index in enumerate(order):
+        slot = place % depth
+        if place >= depth - 1:
+            store(place - depth + 1, 0, columns).wait()
+        if place + 1 < tiles and order[place + 1] >= early:
+            fetch(place + 1).start()
         if close:
-            tall = rows_ref[:, rows_of(index)].T
+            tall = rows_ref[:, index * tile : (index + 1) * tile].T
         else:
-            fetch_rows(index).wait()
-            tall = rows_buf[slot].T
+            fetch_rows(place).start()
+            fetch_rows(place).wait()
+            tall = rows_buf[...].T
+        if index >= early:
+            fetch(place).wait()
         total = jnp.zeros((tile, LANES), jnp.float32)
-        for start in range(0, columns, width):
-            gradient = jnp.dot(tall, slope_ref[:, start : start + width], preferred_element_type=jnp.float32)
-            new_buf[slot, :, start : start + width] = BETA * old(start) + mix * gradient * gradient
-            product = weight_buf[slot, :, start : start + width].astype(jnp.float32) * gradient
+        for n, weight_ref in enumerate(weight_refs):
+            where = slice(n * width, (n + 1) * width)
+            gradient = jnp.dot(tall, slope_ref[:, where], preferred_element_type=jnp.float32)
+            old = early_refs[index][:, where] if index < early else slab[slot, :, where]
+            slab[slot, :, where] = BETA * old + mix * gradient * gradient
+            product = weight_ref[index * tile : (index + 1) * tile, :].astype(jnp.float32) * gradient
             for lane in range(0, width, LANES):
                 total = total + product[:, lane : lane + LANES]
-        gain_ref[:, rows_of(index)] = jnp.sum(total.T, axis=0, keepdims=True)
-        store(index).start()
-
-        @pl.when(index + 2 < tiles)
-        def _():
-            fetch_weight(index + 2).start()
-            if not close:
-                fetch_rows(index + 2).start()
-
-    for index in range(min(2, tiles)):
-        fetch_weight(index).start()
-        if not close:
-            fetch_rows(index).start()
-    for index in range(early, min(early + 2, tiles)):
-        fetch(index).start()
-
-    @pl.loop(0, early)
-    def _(index):
-        work(index, lambda start: early_ref[rows_of(index), start : start + width])
-
-    @pl.loop(early, tiles)
-    def _(index):
-        fetch(index).wait()
-        work(index, lambda start: ema_buf[lax.rem(index, 2), :, start : start + width])
-
-        @pl.when(index + 2 < tiles)
-        def _():
-            fetch(index + 2).start()
-
-    for index in range(max(tiles - 2, 0), tiles):
-        store(index).wait()
-
-
-def head_update(rows, slope, early, head_weight, head_ema, tile, close, limit):
+            store(place, n * width, width).start()
+        gain_ref[:, index * tile : (index + 1) * tile] = jnp.sum(total.T, axis=0, keepdims=True)
+    for place in range(max(tiles - depth + 1, 0), tiles):
+        store(place, 0, columns).wait()
+
+
+def head_update(rows, slope, weights, early, head_ema, tile, close, limit):
     features, columns = head_ema.shape
     anywhere = pl.BlockSpec(memory_space=pl.ANY)
     near = pl.BlockSpec(memory_space=pltpu.VMEM)
     dma = pltpu.SemaphoreType.DMA
     return pl.pallas_call(
-        functools.partial(update_kernel, tile, close),
+        functools.partial(update_kernel, tile, close, len(early)),
         out_shape=(
             jax.ShapeDtypeStruct((features, columns), jnp.float32),
             jax.ShapeDtypeStruct((1, features), jnp.float32),
         ),
-        in_specs=[near if close else anywhere, near, near, anywhere, anywhere],
+        in_specs=[anywhere, near if close else anywhere] + [near] * (1 + len(weights) + len(early)),
         out_specs=(anywhere, near),
         scratch_shapes=[
-            pltpu.VMEM((2, 16, LANES) if close else (2, rows.shape[0], tile), jnp.bfloat16),
-            pltpu.VMEM((2, tile, columns), jnp.bfloat16),
-            pltpu.VMEM((2, tile, columns), jnp.float32),
-            pltpu.VMEM((2, tile, columns), jnp.float32),
-        ]
-        + [dma((2,))] * 4,
+            pltpu.VMEM((16, LANES) if close else (rows.shape[0], tile), jnp.bfloat16),
+            pltpu.VMEM((3, tile, columns), jnp.float32),
+            dma,
+            dma((3,)),
+            dma((3,)),
+        ],
         compiler_params=pltpu.CompilerParams(vmem_limit_bytes=limit),
         name="head_update",
-    )(rows, slope, early, head_weight, head_ema)
+    )(head_ema, rows, slope, *weights, *early)
 
 
 def exchange_kernel(parts, ways, x_ref, y_ref, part_slots, way_slots, half, send_sem, part_sem, way_sem):
@@ -615,13 +597,13 @@
     tile = 512 if features % 512 == 0 else 256
     slab = tile * columns * 4
     close = count * features * 2 <= 12 * MIB
-    limit = max(features * columns * 2 + count * (columns + 4 * LANES) * 4, 5 * slab) + 4 * MIB
-    room = 52 * MIB - limit - count * (features + columns) * 2
-    early = min(max(room // slab, 1), features // tile) * tile
-    rows, slope, early_ema = forward(
-        hidden.reshape(own, features), norm_gain.reshape(1, features), labels.reshape(1, own), head_weight, head_ema, parts, ways, early, limit
+    limit = max(count * (columns + 4 * LANES) * 4, 3 * slab + (0 if close else count * tile * 2)) + 3 * MIB
+    room = 53 * MIB - limit - count * (features + columns) * 2 - features * columns * 2
+    early = min(max(room // slab, 0), features // tile)
+    rows, slope, *kept = forward(
+        hidden.reshape(own, features), norm_gain.reshape(1, features), labels, head_weight, head_ema, parts, ways, early, tile, limit
     )
-    head_new, partial_sum = head_update(rows, slope, early_ema, head_weight, head_ema, tile, close, limit)
+    head_new, partial_sum = head_update(rows, slope, kept[:PIECES], kept[PIECES:], head_ema, tile, close, limit)
     gain_grad = exchange(partial_sum, parts, ways).reshape(features) / norm_gain.astype(jnp.float32)
     gain_new = BETA * gain_ema + (1.0 - BETA) * gain_grad * gain_grad / count
     return (head_new, gain_new)

time: 97.5 us -> 90.7 us (0.930)
  Pallas kernels: 93.3 us -> 86.4 us
    pallas_call x2, Pallas kernels: 83.5 us -> 77.2 us  [the longest x1 52.5 us: forward(): pl.pallas_call(functools.partial(forward_kernel, parts, ways, early), out...]
where the time goes in v2:
time: 90.7 us; the launch traced here: 90.3 us
  Pallas kernels  86.4 us (95%)
  local copies, waits for them, and re-layouts  2.53 us (3%)
    pallas_call x1, Pallas kernels, forward(): pl.pallas_call(functools.partial(forward_kernel, parts, ways, early), out...  52.5 us
    pallas_call x1, Pallas kernels, head_update(): pl.pallas_call(functools.partial(update_kernel, tile, close, len(early)),...  24.7 us
    pallas_call x1, Pallas kernels, exchange(): pl.pallas_call(functools.partial(exchange_kernel, parts, ways), out_shape...  9.23 us
    unnamed x8, local copies, waits for them, and re-layouts  1.82 us

profile of v2, /device:TPU:0, one launch (start us, length us, event | category | flops | bytes accessed | tf_op | source)
XLA Modules:
  0.0 90.3 jit_solution(10460570203243877807)
XLA Ops:
  0.6 0.7 reshape.14.gain_ref
  1.3 0.0 copy-start
  1.4 1.1 %copy-done = bf16[2,48,4096]{2,1,0:T(8,128)(2,1)S(1)} copy-done((bf16[2,48,4096]{2,1,0:T(8,128)(2,1)S(1)}, bf16[2,48,4096]{2,1,0:T(8,128)(2,1)}, u32[]{:S(2)}) %copy-start) | copy-done | bytes 786456
  2.5 0.0 copy-start.1
  2.5 0.7 copy-done.1
  3.2 52.5 %forward.1 = (bf16[768,4096]{1,0:T(8,128)(2,1)S(1)}, bf16[768,2048]{1,0:T(8,128)(2,1)S(1)}, bf16[4096,512]{1,0:T(8,128)(2,1)S(1)}, bf16[4096,512]{1,0:T(8,128)(2...) custom-call(bf16[96,4096]{1,0:T(8,128)(2,1)S(1)} %bitcast.2, ...), custom_call_target="tpu_custom_call" | custom-call | tf_op jit(solution)/shard_map/forward/pallas_call | solution.py:390
  55.6 0.0 copy-start.2
  55.7 0.0 copy-start.3
  55.7 24.7 %head_update.1 = (f32[4096,2048]{1,0:T(8,128)}, f32[1,4096]{1,0:T(1,128)S(1)}) custom-call(f32[4096,2048]{1,0:T(8,128)} %ema_hbm.3, bf16[768,4096]{1,0:T(8,128)(2,1)S(1)} %get-tuple-element.13.rows_ref, bf16[768,2048]{1,0:T(8,128)(2,1)S(1)} %get-tuple-element.14.slope_ref, bf16[4096,512]{1,0:T(8,128)(2,1)S(1)} %get-tuple-element.15.refs_0_, ...), custom_call_target="tpu_custom_call" | custom-call | tf_op jit(solution)/shard_map/head_update/pallas_call | solution.py:493
  80.4 9.2 %exchange_gain.1 = f32[1,4096]{1,0:T(1,128)S(1)} custom-call(f32[1,4096]{1,0:T(1,128)S(1)} %get-tuple-element.23.x_ref), custom_call_target="tpu_custom_call" | custom-call | tf_op jit(solution)/shard_map/exchange_gain/pallas_call | solution.py:574
  89.7 0.0 copy-done.2
  89.7 0.0 copy-done.3
  89.7 0.6 fusion.1
Async XLA Ops:
  1.3 1.1 %copy-start = (bf16[2,48,4096]{2,1,0:T(8,128)(2,1)S(1)}, bf16[2,48,4096]{2,1,0:T(8,128)(2,1)}, u32[]{:S(2)}) copy-start(bf16[2,48,4096]{2,1,0:T(8,128)(2,1)} %param.6) | copy-start | bytes 2359300
  2.5 0.7 copy-start.1
  55.6 34.0 %copy-start.2 = (bf16[4096]{0:T(1024)(128)(2,1)S(1)}, bf16[4096]{0:T(1024)(128)(2,1)}, u32[]{:S(2)}) copy-start(bf16[4096]{0:T(1024)(128)(2,1)} %param.7) | copy-start | bytes 24580
  55.7 34.0 %copy-start.3 = (f32[4096]{0:T(1024)S(1)}, f32[4096]{0:T(1024)}, u32[]{:S(2)}) copy-start(f32[4096]{0:T(1024)} %param.11) | copy-start | bytes 49156

commit v3 on v2

--- a/solution.py
+++ b/solution.py
@@ -434,12 +434,9 @@
     depth = slab.shape[0]
     mix = (1.0 - BETA) / count
     width = columns // PIECES
-    late = list(range(early, tiles))
-    order = []
-    for index in range(early):
-        order += [index] + late[:1]
-        late = late[1:]
-    order += late
+    late = iter(range(early, tiles))
+    early_at = {tiles * index // early: index for index in range(early)} if early else {}
+    order = [early_at[place] if place in early_at else next(late) for place in range(tiles)]
 
     def fetch(place):
         slot = place % depth

time: 90.7 us -> 90.1 us (level)
  no operation moved by 1% of the time
where the time goes in v3:
time: 90.1 us; the launch traced here: 89.8 us
  Pallas kernels  85.9 us (95%)
  local copies, waits for them, and re-layouts  2.53 us (3%)
    pallas_call x1, Pallas kernels, forward(): pl.pallas_call(functools.partial(forward_kernel, parts, ways, early), out...  52.5 us
    pallas_call x1, Pallas kernels, head_update(): pl.pallas_call(functools.partial(update_kernel, tile, close, len(early)),...  24.2 us
    pallas_call x1, Pallas kernels, exchange(): pl.pallas_call(functools.partial(exchange_kernel, parts, ways), out_shape...  9.23 us
    unnamed x8, local copies, waits for them, and re-layouts  1.82 us

profile of v3, /device:TPU:0, one launch (start us, length us, event | category | flops | bytes accessed | tf_op | source)
XLA Modules:
  0.0 89.8 jit_solution(7742572783303388920)
XLA Ops:
  0.6 0.7 reshape.14.gain_ref
  1.3 0.0 copy-start
  1.4 1.1 %copy-done = bf16[2,48,4096]{2,1,0:T(8,128)(2,1)S(1)} copy-done((bf16[2,48,4096]{2,1,0:T(8,128)(2,1)S(1)}, bf16[2,48,4096]{2,1,0:T(8,128)(2,1)}, u32[]{:S(2)}) %copy-start) | copy-done | bytes 786456
  2.5 0.0 copy-start.1
  2.5 0.7 copy-done.1
  3.2 52.5 %forward.1 = (bf16[768,4096]{1,0:T(8,128)(2,1)S(1)}, bf16[768,2048]{1,0:T(8,128)(2,1)S(1)}, bf16[4096,512]{1,0:T(8,128)(2,1)S(1)}, bf16[4096,512]{1,0:T(8,128)(2...) custom-call(bf16[96,4096]{1,0:T(8,128)(2,1)S(1)} %bitcast.2, ...), custom_call_target="tpu_custom_call" | custom-call | tf_op jit(solution)/shard_map/forward/pallas_call | solution.py:390
  55.6 0.0 copy-start.2
  55.7 0.0 copy-start.3
  55.7 24.2 %head_update.1 = (f32[4096,2048]{1,0:T(8,128)}, f32[1,4096]{1,0:T(1,128)S(1)}) custom-call(f32[4096,2048]{1,0:T(8,128)} %ema_hbm.3, bf16[768,4096]{1,0:T(8,128)(2,1)S(1)} %get-tuple-element.13.rows_ref, bf16[768,2048]{1,0:T(8,128)(2,1)S(1)} %get-tuple-element.14.slope_ref, bf16[4096,512]{1,0:T(8,128)(2,1)S(1)} %get-tuple-element.15.refs_0_, ...), custom_call_target="tpu_custom_call" | custom-call | tf_op jit(solution)/shard_map/head_update/pallas_call | solution.py:490
  79.9 9.2 %exchange_gain.1 = f32[1,4096]{1,0:T(1,128)S(1)} custom-call(f32[1,4096]{1,0:T(1,128)S(1)} %get-tuple-element.23.x_ref), custom_call_target="tpu_custom_call" | custom-call | tf_op jit(solution)/shard_map/exchange_gain/pallas_call | solution.py:571
  89.1 0.0 copy-done.2
  89.1 0.0 copy-done.3
  89.1 0.6 fusion.1
Async XLA Ops:
  1.3 1.1 %copy-start = (bf16[2,48,4096]{2,1,0:T(8,128)(2,1)S(1)}, bf16[2,48,4096]{2,1,0:T(8,128)(2,1)}, u32[]{:S(2)}) copy-start(bf16[2,48,4096]{2,1,0:T(8,128)(2,1)} %param.6) | copy-start | bytes 2359300
  2.5 0.7 copy-start.1
  55.6 33.5 %copy-start.2 = (bf16[4096]{0:T(1024)(128)(2,1)S(1)}, bf16[4096]{0:T(1024)(128)(2,1)}, u32[]{:S(2)}) copy-start(bf16[4096]{0:T(1024)(128)(2,1)} %param.7) | copy-start | bytes 24580
  55.7 33.5 %copy-start.3 = (f32[4096]{0:T(1024)S(1)}, f32[4096]{0:T(1024)}, u32[]{:S(2)}) copy-start(f32[4096]{0:T(1024)} %param.11) | copy-start | bytes 49156
